TPU v7x, 32 devices: a whole 2x2x4 slice. The times are simulated.
32 devices in a mesh: ctx: 8 (over z, y), chan: 4 (over x, core).
Axes of the slice: x: 2, y: 2, z: 4, core: 2. Of those that a mesh axis runs over, the one named last changes fastest.
Arguments:
- tokens: bfloat16 [2048, 4096], P('ctx', 'chan'), may hold values from -6 to 6
- gain: float32 [4096], replicated, may hold values from 0.1 to 1.9
- in_weight: bfloat16 [3, 4096, 2048], P(None, None, 'chan'), may hold values from -0.09375 to 0.09375
- short_weight: float32 [3, 3, 2048], P(None, None, 'chan'), may hold values from -3.5 to 3.5
- residues: float32 [16, 2048], P(None, 'chan'), may hold values from -1.5 to 1.5
- rates: float32 [16, 2048], P(None, 'chan'), may hold values from 0.1 to 51
- out_weight: bfloat16 [2048, 4096], P('chan'), may hold values from -0.1875 to 0.1875
Outputs:
- mixed: bfloat16 [2048, 4096], P('ctx', 'chan')
All inputs are finite; a program needn't handle non-finite values.
Results may differ from a plain program's by a relative error of at most 0.018.
Values may be sent and summed in bfloat16 or wider, within the bound.
A program may use at most 128 MiB of HBM per device.

v0:
```python
import math
import jax
import jax.numpy as jnp
from jax import lax
from jax.sharding import PartitionSpec as P

highest = lax.Precision.HIGHEST
two_pi = 2.0 * math.pi


def shortened(shard):

    def short(part):
        return part.astype(jnp.bfloat16) if part.dtype == jnp.float32 else part

    return jax.tree.map(short, shard)


def from_behind(shard, axis, by):
    peers = lax.axis_size(axis)
    pairs = [(i, i + by) for i in range(peers) if 0 <= i + by < peers]
    return lax.ppermute(shard, axis, pairs)


def turn_angle(first, second, modulus):
    return (first * second % modulus).astype(jnp.float32) * (two_pi / modulus)


def local_forward(spectra, freq_slots, padded_length):
    row_count = spectra.shape[3]
    steps_idx = jnp.arange(row_count, dtype=jnp.int32)
    twiddle = turn_angle(freq_slots[:, None], steps_idx[None, :], padded_length)[:, :, None]
    cosine_term = jnp.cos(twiddle)
    sine_term = jnp.sin(twiddle)
    real_part = spectra[:, 0]
    imag_part = spectra[:, 1]
    turned_real = real_part * cosine_term + imag_part * sine_term
    turned_imag = imag_part * cosine_term - real_part * sine_term
    stacked = jnp.concatenate([turned_real, turned_imag], axis=2)
    dft_angle = turn_angle(steps_idx[:, None], steps_idx[None, :], row_count)
    cos_table = jnp.cos(dft_angle)
    sin_table = jnp.sin(dft_angle)
    block_table = jnp.concatenate(
        [
            jnp.concatenate([cos_table, sin_table], axis=1),
            jnp.concatenate([-sin_table, cos_table], axis=1),
        ],
        axis=0,
    )
    both_parts = jnp.einsum("pj,fsjc->fspc", block_table, stacked, precision=highest)
    return (both_parts[:, :, :row_count], both_parts[:, :, row_count:])


def local_inverse(spec_real, spec_imag, freq_slots, padded_length):
    row_count = spec_real.shape[1]
    steps_idx = jnp.arange(row_count, dtype=jnp.int32)
    dft_angle = turn_angle(steps_idx[:, None], steps_idx[None, :], row_count)
    cos_table = jnp.cos(dft_angle)
    sin_table = jnp.sin(dft_angle)
    block_table = jnp.concatenate(
        [
            jnp.concatenate([cos_table, -sin_table], axis=1),
            jnp.concatenate([sin_table, cos_table], axis=1),
        ],
        axis=0,
    )
    stacked = jnp.concatenate([spec_real, spec_imag], axis=1)
    both_parts = jnp.einsum("jp,spc->sjc", block_table, stacked, precision=highest) / row_count
    back_real = both_parts[:, :row_count]
    back_imag = both_parts[:, row_count:]
    twiddle = turn_angle(freq_slots[:, None], steps_idx[None, :], padded_length)[:, :, None]
    cosine_term = jnp.cos(twiddle)
    sine_term = jnp.sin(twiddle)
    return (
        back_real * cosine_term - back_imag * sine_term,
        back_imag * cosine_term + back_real * sine_term,
    )


def across_blocks(received, sample_ids, freq_count):
    freq_ids = jnp.arange(freq_count, dtype=jnp.int32)
    rotation = turn_angle(freq_ids[:, None], sample_ids[None, :], freq_count)
    real_part = jnp.einsum("qm,fmjc->fqjc", jnp.cos(rotation), received, precision=highest)
    imag_part = -jnp.einsum("qm,fmjc->fqjc", jnp.sin(rotation), received, precision=highest)
    return jnp.stack([real_part, imag_part], axis=1)


def rows_from_spectra(received, sample_ids, freq_count):
    freq_ids = jnp.arange(freq_count, dtype=jnp.int32)
    rotation = turn_angle(sample_ids[:, None], freq_ids[None, :], freq_count)
    real_rows = jnp.einsum("mq,qjc->mjc", jnp.cos(rotation), received[0], precision=highest)
    real_rows = real_rows - jnp.einsum(
        "mq,qjc->mjc", jnp.sin(rotation), received[1], precision=highest
    )
    return real_rows / freq_count


def halved_forward(signal, device_index, group_size):
    received = lax.all_to_all(
        signal[:, None].astype(jnp.bfloat16), "ctx", split_axis=2, concat_axis=1, tiled=True
    ).astype(jnp.float32)
    spectra = across_blocks(received, jnp.arange(group_size, dtype=jnp.int32), 2 * group_size)
    gathered = lax.all_to_all(
        shortened(spectra), "ctx", split_axis=2, concat_axis=3, tiled=True
    ).astype(spectra.dtype)
    return (gathered, 2 * device_index + jnp.arange(2, dtype=jnp.int32))


def halved_inverse(spec_real, spec_imag, group_size):
    received = lax.all_to_all(
        shortened(jnp.stack([spec_real, spec_imag], axis=0)),
        "ctx",
        split_axis=2,
        concat_axis=1,
        tiled=True,
    )
    real_rows = rows_from_spectra(received, jnp.arange(group_size, dtype=jnp.int32), 2 * group_size)
    returned = lax.all_to_all(
        shortened(real_rows), "ctx", split_axis=0, concat_axis=1, tiled=True
    ).astype(real_rows.dtype)
    return returned[0]


def shards(tokens, gain, in_weight, short_weight, residues, rates, out_weight):
    features_all = lax.all_gather(tokens, "chan", axis=1, tiled=True)
    wide_rows = features_all.astype(jnp.float32)
    scale_rms = lax.rsqrt(jnp.mean(wide_rows * wide_rows, axis=-1, keepdims=True) + 1e-06)
    normed = (wide_rows * scale_rms * gain).astype(jnp.bfloat16)
    projected = jnp.einsum(
        "td,gdc->gtc", normed, in_weight, preferred_element_type=jnp.float32
    ).astype(jnp.bfloat16)
    row_count = projected.shape[1]
    rim_size = short_weight.shape[1] - 1
    rim_rows = from_behind(projected[:, row_count - rim_size :, :], "ctx", 1)
    extended = jnp.concatenate([rim_rows, projected], axis=1).astype(jnp.float32)
    filtered = jnp.zeros((3, row_count, projected.shape[2]), jnp.float32)
    for i in range(rim_size + 1):
        filtered = (
            filtered
            + short_weight[:, i][:, None, :] * extended[:, rim_size - i : rim_size - i + row_count]
        )
    drive_term = filtered[1] * filtered[2]
    group_size = lax.axis_size("ctx")
    device_index = lax.axis_index("ctx")
    length = row_count * group_size
    padded_length = 2 * length
    decay_rate = rates / length
    amplitude = residues * jnp.sqrt(-jnp.expm1(-2.0 * decay_rate))
    positions = (device_index * row_count + jnp.arange(row_count, dtype=jnp.int32)).astype(
        jnp.float32
    )
    kernel = jnp.sum(
        amplitude[:, None, :] * jnp.exp(-decay_rate[:, None, :] * positions[None, :, None]), axis=0
    )
    signal = jnp.stack([drive_term, kernel], axis=0)
    spectra, freq_slots = halved_forward(signal, device_index, group_size)
    spec_real, spec_imag = local_forward(spectra, freq_slots, padded_length)
    resp_real = spec_real[1]
    resp_imag = spec_imag[1]
    prod_real = spec_real[0] * resp_real - spec_imag[0] * resp_imag
    prod_imag = spec_real[0] * resp_imag + spec_imag[0] * resp_real
    back_real, back_imag = local_inverse(prod_real, prod_imag, freq_slots, padded_length)
    convolved = halved_inverse(back_real, back_imag, group_size)
    gated_rows = (filtered[0] * convolved).astype(jnp.bfloat16)
    partial_sums = jnp.dot(gated_rows, out_weight, preferred_element_type=jnp.float32)
    return lax.psum_scatter(
        partial_sums.astype(jnp.bfloat16), "chan", scatter_dimension=1, tiled=True
    )


def solution(mesh):
    return jax.shard_map(
        shards,
        mesh=mesh,
        in_specs=(
            P("ctx", "chan"),
            P(),
            P(None, None, "chan"),
            P(None, None, "chan"),
            P(None, "chan"),
            P(None, "chan"),
            P("chan", None),
        ),
        out_specs=P("ctx", "chan"),
        check_vma=False,
    )
```

profile of v0, /device:TPU:0, one launch (start us, length us, event | category | flops | bytes accessed | tf_op | source)
XLA Modules:
  0.0 229.2 jit_solution(4837787021221969557)
XLA Ops:
  6.5 0.7 all-gather.2.cloned.1.call-update
  7.3 0.9 fusion.110
  8.1 0.8 sqrt_multiply_fusion
  9.0 1.4 multiply_reduce_fusion
  10.4 23.8 %all-gather.2.cloned.1.call-done = bf16[256,4096]{1,0:T(8,128)(2,1)} async-done(((bf16[256,1024]{1,0:T(8,128)(2,1)}), bf16[256,4096]{1,0:T(8,128)(2,1)}) %all-gather.2.cloned.1.call-update) | async-done | bytes 2097168 | tf_op jit(solution)/shard_map/all_gather | solution.py:125
  34.2 2.2 fusion
  36.5 6.6 %fusion.28 = bf16[3,256,512]{2,1,0:T(8,128)(2,1)S(1)} fusion(bf16[3,4096,512]{2,1,0:T(8,128)(2,1)} %param.9, bf16[256,4096]{1,0:T(8,128)(2,1)S(1)} %copy-done.2, f32[4096]{0:T(1024)S(1)} %copy-done.3, f32[256]{0:T(256)S(1)} %add_rsqrt_fusion), kind=kOutput, calls=%fused_computation.40 | convolution fusion | flops 3225812992 | bytes 15483904 | tf_op jit(solution)/shard_map/td,gdc->gtc/dot_general | solution.py:129
  43.1 3.4 %collective-permute-start = (bf16[3,2,512]{2,1,0:T(2,128)(2,1)S(1)}, bf16[3,2,512]{2,1,0:T(2,128)(2,1)S(1)}, u32[]{:S(2)}, u32[]{:S(2)}) collective-permute-start(bf16[3,2,512]{2,1,0:T(2,128)(2,1)S(1)} %slice.90), channel_id=1, source_target_pairs={{0,4},{4,8},{8,12},{12,16},{16,20},{20,24},{24,28},{1,5},{5,9},{9,... | collective-permute-start | bytes 18440 | tf_op jit(solution)/shard_map/ppermute | solution.py:22
  46.5 1.3 collective-permute-done
  47.8 0.2 maximum_convert_fusion
  48.1 0.5 fusion.21
  48.6 0.1 fusion.54
  48.6 0.1 pad_maximum_fusion.8
  48.7 0.5 copy.56
  49.2 19.9 %all_to_all.45 = bf16[2,1,256,512]{3,0,1,2:T(2,128)(2,1)S(1)} all-to-all(bf16[2,1,256,512]{3,0,1,2:T(2,128)(2,1)S(1)} %copy.56), channel_id=1, replica_groups=mesh['ctx'=8,'chan'=4] {'ctx'}, dimensions={2} | all-to-all | bytes 1048576 | tf_op jit(solution)/shard_map/all_to_all | solution.py:99
  69.1 0.1 copy.57
  69.2 1.1 fusion.26
  70.3 1.1 fusion.27
  71.4 0.2 pad_maximum_fusion
  71.6 2.5 %copy.60 = bf16[2,2,16,32,512]{4,3,0,1,2:T(8,128)(2,1)} copy(bf16[2,2,16,32,512]{4,2,3,0,1:T(8,128)(2,1)S(1)} %pad_maximum_fusion) | data formatting | bytes 4194304 | tf_op jit(solution)/shard_map/stack | solution.py:85
  74.1 3.6 %all-to-all-start.1 = ((bf16[2,2,16,32,512]{4,3,0,1,2:T(8,128)(2,1)}), bf16[2,2,16,32,512]{4,3,0,1,2:T(8,128)(2,1)S(1)}, u32[]{:S(2)}, u32[]{:S(2)}) async-start(bf16[2,2,16,32,512]{4,3,0,1,2:T(8,128)(2,1)} %copy.60), calls=%async_computation.1 | async-start | bytes 4194304 | tf_op jit(solution)/shard_map/all_to_all | solution.py:103
  77.8 0.2 reduce-scatter.2.cloned.1.call-start
  78.0 1.0 fusion.60
  79.0 1.0 fusion.58
  80.0 0.1 fusion.90
  80.2 45.4 %all-to-all-done.1 = bf16[2,2,16,32,512]{4,3,0,1,2:T(8,128)(2,1)S(1)} async-done(((bf16[2,2,16,32,512]{4,3,0,1,2:T(8,128)(2,1)}), bf16[2,2,16,32,512]{4,3,0,1,2:T(8,128)(2,1)S(1)}, u32[]{:S(2)}, u32[]{:S(2)}) %all-to-all-start.1) | async-done | bytes 2097184 | tf_op jit(solution)/shard_map/all_to_all | solution.py:103
  125.5 0.6 copy.61
  126.1 0.5 multiply_add_fusion
  126.6 7.9 %fusion.7 = f32[2,2,512,512]{3,2,1,0:T(8,128)S(1)} fusion(f32[2,2,256,512]{3,2,1,0:T(8,128)S(1)} %get-tuple-element.6, f32[2,2,256,512]{3,2,1,0:T(8,128)S(1)} %get-tuple-element.5, f32[256,256]{1,0:T(8,128)S(1)} %get-tuple-element.23, f32[256,256]{1,0:T(8,128)S(1)} %fusion.60, f32[256,256]{1,0:T(8,128)S(1)} %get-tuple-element.22), kind=kOutput, calls=%fused_computation.11 | convolution fusion | flops 6444285952 | bytes 9175040 | tf_op jit(solution)/shard_map/pj,fsjc->fspc/dot_general | solution.py:50
  134.6 0.5 subtract_bitcast_fusion
  135.1 7.1 %multiply_bitcast_fusion = f32[2,512,512]{1,2,0:T(8,128)S(1)} fusion(f32[2,256,512]{2,1,0:T(8,128)S(1)} %get-tuple-element.8, f32[2,256,512]{2,1,0:T(8,128)S(1)} %get-tuple-element.7, f32[256,256]{1,0:T(8,128)S(1)} %get-tuple-element.23, f32[256,256]{1,0:T(8,128)S(1)} %get-tuple-element.22, f32[256,256]{1,0:T(8,128)S(1)} %fusion.60), kind=kOutput, calls=%fused_computation.21 | convolution fusion | flops 3223060480 | bytes 4980736 | tf_op jit(solution)/shard_map/jp,spc->sjc/dot_general | solution.py:68
  142.2 0.3 fusion.43
  142.5 0.1 pad_maximum_fusion.7
  142.6 1.1 copy.63
  143.7 29.3 %all_to_all.46 = bf16[2,2,256,512]{3,1,0,2:T(2,128)(2,1)S(1)} all-to-all(bf16[2,2,256,512]{3,1,0,2:T(2,128)(2,1)S(1)} %copy.63), channel_id=1, replica_groups=mesh['ctx'=8,'chan'=4] {'ctx'}, dimensions={2} | all-to-all | bytes 2097152 | tf_op jit(solution)/shard_map/all_to_all | solution.py:110
  173.1 0.2 copy.64
  173.3 0.1 fusion.109
  173.4 0.5 copy.65
  173.9 0.2 squeeze.13
  174.1 0.4 fusion.70
  174.6 0.5 copy.66
  175.1 0.2 squeeze.28
  175.3 0.4 fusion.32
  175.7 0.1 copy.67
  175.8 12.0 %all_to_all.47 = bf16[8,32,512]{2,1,0:T(8,128)(2,1)S(1)} all-to-all(bf16[8,32,512]{2,1,0:T(8,128)(2,1)S(1)} %copy.67), channel_id=1, replica_groups=mesh['ctx'=8,'chan'=4] {'ctx'}, dimensions={0} | all-to-all | bytes 524288 | tf_op jit(solution)/shard_map/all_to_all | solution.py:118
  187.8 4.8 %convolution_convert_fusion = bf16[256,4096]{1,0:T(8,128)(2,1)} fusion(bf16[512,4096]{1,0:T(8,128)(2,1)} %param.13, f32[3,256,512]{2,1,0:T(8,128)S(1)} %copy-done.1, bf16[256,512]{1,0:T(8,128)(2,1)S(1)} %bitcast.108), kind=kOutput, calls=%fused_computation.3 | convolution fusion | flops 1075183616 | bytes 7077888 | tf_op jit(solution)/shard_map/dot_general | solution.py:165
  192.6 0.0 reduce-scatter.2.cloned.1.call-update
  192.6 29.7 %reduce-scatter.2.cloned.1.call-done = bf16[256,1024]{1,0:T(8,128)(2,1)} async-done(((bf16[256,4096]{1,0:T(8,128)(2,1)}), bf16[256,1024]{1,0:T(8,128)(2,1)}) %reduce-scatter.2.cloned.1.call-update) | async-done | bytes 524304 | tf_op jit(solution)/shard_map/reduce_scatter | solution.py:166
  (15 shorter events, 0.1 us)
Async XLA Ops:
  6.5 27.7 %all-gather.2.cloned.1.call-start = ((), (), s32[]{:S(2)}) async-start(), calls=%async_computation.5 | async-start | bytes 2621440 | tf_op jit(solution)/shard_map/all_gather | solution.py:125
  9.0 27.5 %copy-start.3 = (f32[4096]{0:T(1024)S(1)}, f32[4096]{0:T(1024)}, u32[]{:S(2)}) copy-start(f32[4096]{0:T(1024)} %param.8) | copy-start | bytes 49156
  34.2 2.3 copy-start.2
  43.1 4.7 %collective-permute-start = (bf16[3,2,512]{2,1,0:T(2,128)(2,1)S(1)}, bf16[3,2,512]{2,1,0:T(2,128)(2,1)S(1)}, u32[]{:S(2)}, u32[]{:S(2)}) collective-permute-start(bf16[3,2,512]{2,1,0:T(2,128)(2,1)S(1)} %slice.90), channel_id=1, source_target_pairs={{0,4},{4,8},{8,12},{12,16},{16,20},{20,24},{24,28},{1,5},{5,9},{9,... | collective-permute-start | bytes 18440 | tf_op jit(solution)/shard_map/ppermute | solution.py:22
  48.5 20.6 %copy-start = (f32[3,256,512]{2,1,0:T(8,128)}, f32[3,256,512]{2,1,0:T(8,128)S(1)}, u32[]{:S(2)}) copy-start(f32[3,256,512]{2,1,0:T(8,128)S(1)} %fusion.21) | copy-start | bytes 4718596
  74.1 51.4 %all-to-all-start.1 = ((bf16[2,2,16,32,512]{4,3,0,1,2:T(8,128)(2,1)}), bf16[2,2,16,32,512]{4,3,0,1,2:T(8,128)(2,1)S(1)}, u32[]{:S(2)}, u32[]{:S(2)}) async-start(bf16[2,2,16,32,512]{4,3,0,1,2:T(8,128)(2,1)} %copy.60), calls=%async_computation.1 | async-start | bytes 4194304 | tf_op jit(solution)/shard_map/all_to_all | solution.py:103
  77.8 144.6 %reduce-scatter.2.cloned.1.call-start = ((), (), s32[]{:S(2)}) async-start(), calls=%async_computation.6 | async-start | bytes 2621440 | tf_op jit(solution)/shard_map/reduce_scatter | solution.py:166
  174.6 13.3 %copy-start.1 = (f32[3,256,512]{2,1,0:T(8,128)S(1)}, f32[3,256,512]{2,1,0:T(8,128)}, u32[]{:S(2)}) copy-start(f32[3,256,512]{2,1,0:T(8,128)} %copy-done) | copy-start | bytes 4718596
Sparse Core Ops, SparseCore 0:
  8.9 25.2 all-gather.1
  192.8 29.5 reduce-scatter.1
where the time goes:
time: 230 us; the launch traced here: 229 us
  waiting for transfers between devices  101 us (44%)
  blocking collectives  61.2 us (27%)
  matrix products  29.5 us (13%)
  between operations  13.7 us (6%)
  other arithmetic  9.09 us (4%)
  local copies, waits for them, and re-layouts  7.54 us (3%)
  starting transfers between devices  7.23 us (3%)
    all_to_all x1, waiting for transfers between devices, halved_forward(): lax.all_to_all(shortened(spectra), 'ctx', split_axis=2, concat_axis=3, ti...  45.4 us
    reduce_scatter x1, waiting for transfers between devices, shards(): lax.psum_scatter(partial_sums.astype(jnp.bfloat16), 'chan', scatter_dimen...  29.7 us
    all_to_all x1, blocking collectives, halved_inverse(): lax.all_to_all(shortened(jnp.stack([spec_real, spec_imag], axis=0)), 'ctx...  29.3 us
    all_gather x1, waiting for transfers between devices, shards(): features_all = lax.all_gather(tokens, 'chan', axis=1, tiled=True)  23.8 us
    all_to_all x1, blocking collectives, halved_forward(): lax.all_to_all(signal[:, None].astype(jnp.bfloat16), 'ctx', split_axis=2,...  19.9 us
    all_to_all x1, blocking collectives, halved_inverse(): lax.all_to_all(shortened(real_rows), 'ctx', split_axis=0, concat_axis=1,...  12 us
    dot_general x1, matrix products, local_forward(): jnp.einsum('pj,fsjc->fspc', block_table, stacked, precision=highest)  7.95 us
    dot_general x1, matrix products, local_inverse(): jnp.einsum('jp,spc->sjc', block_table, stacked, precision=highest)  7.1 us
  transfers between devices with their start and end apart: 4, of which 4 were waited for; matrix products, arithmetic and copies ran while one was open for 2% of the time, Pallas kernels for 0%

commit v1 on v0

--- a/solution.py
+++ b/solution.py
@@ -107,12 +107,20 @@
 
 
 def halved_inverse(spec_real, spec_imag, group_size):
-    received = lax.all_to_all(
-        shortened(jnp.stack([spec_real, spec_imag], axis=0)),
-        "ctx",
-        split_axis=2,
-        concat_axis=1,
-        tiled=True,
+
+    def update_packet(message, device_axis):
+        return jnp.concatenate(
+            lax.all_to_all(
+                jnp.stack(jnp.split(message, lax.psum(1, device_axis), 2), 0),
+                concat_axis=0,
+                axis_name=device_axis,
+                split_axis=0,
+            ),
+            1,
+        )
+
+    received = update_packet(
+        shortened(jnp.stack([spec_real, spec_imag], axis=0)), device_axis="ctx"
     )
     real_rows = rows_from_spectra(received, jnp.arange(group_size, dtype=jnp.int32), 2 * group_size)
     returned = lax.all_to_all(

time: 230 us -> 222 us (0.965)
  matrix products: 29.5 us -> 24.4 us
  local copies, waits for them, and re-layouts: 7.54 us -> 4.77 us
    dot_general x1, matrix products: 7.1 us -> 3.78 us  [local_inverse(): jnp.einsum('jp,spc->sjc', block_table, stacked, precision=highest)]
where the time goes in v1:
time: 222 us
  waiting for transfers between devices  101 us (45%)
  blocking collectives  61.5 us (28%)
  matrix products  24.4 us (11%)
  between operations  13.7 us (6%)
  other arithmetic  9.08 us (4%)
  starting transfers between devices  7.23 us (3%)
  local copies, waits for them, and re-layouts  4.77 us (2%)
    all_to_all x1, waiting for transfers between devices, halved_forward(): lax.all_to_all(shortened(spectra), 'ctx', split_axis=2, concat_axis=3, ti...  45.4 us
    reduce_scatter x1, waiting for transfers between devices, shards(): lax.psum_scatter(partial_sums.astype(jnp.bfloat16), 'chan', scatter_dimen...  29.6 us
    all_to_all x1, blocking collectives, update_packet(): lax.all_to_all(jnp.stack(jnp.split(message, lax.psum(1, device_axis), 2),...  29.6 us
    all_gather x1, waiting for transfers between devices, shards(): features_all = lax.all_gather(tokens, 'chan', axis=1, tiled=True)  23.8 us
    all_to_all x1, blocking collectives, halved_forward(): lax.all_to_all(signal[:, None].astype(jnp.bfloat16), 'ctx', split_axis=2,...  19.9 us
    all_to_all x1, blocking collectives, halved_inverse(): lax.all_to_all(shortened(real_rows), 'ctx', split_axis=0, concat_axis=1,...  12 us
    dot_general x1, matrix products, local_forward(): jnp.einsum('pj,fsjc->fspc', block_table, stacked, precision=highest)  7.95 us
    dot_general x1, matrix products, shards(): jnp.einsum('td,gdc->gtc', normed, in_weight, preferred_element_type=jnp.f...  6.59 us
  transfers between devices with their start and end apart: 4, of which 4 were waited for; matrix products, arithmetic and copies ran while one was open for 2% of the time, Pallas kernels for 0%

profile of v1, /device:TPU:0, one launch (start us, length us, event | category | flops | bytes accessed | tf_op | source)
XLA Modules:
  0.0 221.6 jit_solution(15538116923086063474)
XLA Ops:
  6.5 0.0 all-gather.2.cloned.1.call-start
  6.5 0.7 all-gather.2.cloned.1.call-update
  7.3 0.9 fusion.121
  8.1 0.8 sqrt_multiply_fusion
  9.0 0.0 copy-start.4
  9.0 1.4 multiply_reduce_fusion
  10.4 23.8 %all-gather.2.cloned.1.call-done = bf16[256,4096]{1,0:T(8,128)(2,1)} async-done(((bf16[256,1024]{1,0:T(8,128)(2,1)}), bf16[256,4096]{1,0:T(8,128)(2,1)}) %all-gather.2.cloned.1.call-update) | async-done | bytes 2097168 | tf_op jit(solution)/shard_map/all_gather | solution.py:133
  34.2 2.2 %fusion = f32[256]{0:T(256)S(1)} fusion(bf16[256,4096]{1,0:T(8,128)(2,1)} %all-gather.2.cloned.1.call-done), kind=kLoop, calls=%fused_computation.4 | loop fusion | flops 3145472 | bytes 2098176 | tf_op jit(solution)/shard_map/reduce_sum | solution.py:135
  36.5 0.0 copy-done.4
  36.5 0.0 copy-done.2
  36.5 6.6 %fusion.28 = bf16[3,256,512]{2,1,0:T(8,128)(2,1)S(1)} fusion(bf16[3,4096,512]{2,1,0:T(8,128)(2,1)} %param.9, bf16[256,4096]{1,0:T(8,128)(2,1)S(1)} %copy-done.2, f32[4096]{0:T(1024)S(1)} %copy-done.4, f32[256]{0:T(256)S(1)} %add_rsqrt_fusion), kind=kOutput, calls=%fused_computation.54 | convolution fusion | flops 3225812992 | bytes 15483904 | tf_op jit(solution)/shard_map/td,gdc->gtc/dot_general | solution.py:137
  43.1 3.4 %collective-permute-start = (bf16[3,2,512]{2,1,0:T(2,128)(2,1)S(1)}, bf16[3,2,512]{2,1,0:T(2,128)(2,1)S(1)}, u32[]{:S(2)}, u32[]{:S(2)}) collective-permute-start(bf16[3,2,512]{2,1,0:T(2,128)(2,1)S(1)} %slice.90), channel_id=1, source_target_pairs={{0,4},{4,8},{8,12},{12,16},{16,20},{20,24},{24,28},{1,5},{5,9},{9,... | collective-permute-start | bytes 18440 | tf_op jit(solution)/shard_map/ppermute | solution.py:22
  46.5 1.3 collective-permute-done
  47.8 0.2 maximum_convert_fusion
  48.1 0.5 fusion.21
  48.6 0.1 fusion.57
  48.6 0.1 pad_maximum_fusion.7
  48.7 0.5 copy.44
  49.2 19.9 %all_to_all.35 = bf16[2,1,256,512]{3,0,1,2:T(2,128)(2,1)S(1)} all-to-all(bf16[2,1,256,512]{3,0,1,2:T(2,128)(2,1)S(1)} %copy.44), channel_id=1, replica_groups=mesh['ctx'=8,'chan'=4] {'ctx'}, dimensions={2} | all-to-all | bytes 1048576 | tf_op jit(solution)/shard_map/all_to_all | solution.py:99
  69.1 0.0 copy-done
  69.1 0.1 copy.45
  69.2 1.1 fusion.26
  70.3 1.1 fusion.27
  71.4 0.2 pad_maximum_fusion
  71.6 2.5 %copy.48 = bf16[2,2,16,32,512]{4,3,0,1,2:T(8,128)(2,1)} copy(bf16[2,2,16,32,512]{4,2,3,0,1:T(8,128)(2,1)S(1)} %pad_maximum_fusion) | data formatting | bytes 4194304 | tf_op jit(solution)/shard_map/stack | solution.py:85
  74.1 3.6 %all-to-all-start.1 = ((bf16[2,2,16,32,512]{4,3,0,1,2:T(8,128)(2,1)}), bf16[2,2,16,32,512]{4,3,0,1,2:T(8,128)(2,1)S(1)}, u32[]{:S(2)}, u32[]{:S(2)}) async-start(bf16[2,2,16,32,512]{4,3,0,1,2:T(8,128)(2,1)} %copy.48), calls=%async_computation.1 | async-start | bytes 4194304 | tf_op jit(solution)/shard_map/all_to_all | solution.py:103
  77.8 0.2 reduce-scatter.2.cloned.1.call-start
  78.0 1.0 fusion.72
  79.0 1.0 fusion.70
  80.0 0.1 fusion.101
  80.2 45.4 %all-to-all-done.1 = bf16[2,2,16,32,512]{4,3,0,1,2:T(8,128)(2,1)S(1)} async-done(((bf16[2,2,16,32,512]{4,3,0,1,2:T(8,128)(2,1)}), bf16[2,2,16,32,512]{4,3,0,1,2:T(8,128)(2,1)S(1)}, u32[]{:S(2)}, u32[]{:S(2)}) %all-to-all-start.1) | async-done | bytes 2097184 | tf_op jit(solution)/shard_map/all_to_all | solution.py:103
  125.5 0.6 copy.49
  126.1 0.5 multiply_add_fusion
  126.6 8.0 %fusion.7 = f32[2,2,512,512]{3,2,1,0:T(8,128)S(1)} fusion(f32[2,2,256,512]{3,2,1,0:T(8,128)S(1)} %get-tuple-element.6, f32[2,2,256,512]{3,2,1,0:T(8,128)S(1)} %get-tuple-element.5, f32[256,256]{1,0:T(8,128)S(1)} %get-tuple-element.23, f32[256,256]{1,0:T(8,128)S(1)} %fusion.72, f32[256,256]{1,0:T(8,128)S(1)} %get-tuple-element.22), kind=kOutput, calls=%fused_computation.11 | convolution fusion | flops 6444285952 | bytes 9175040 | tf_op jit(solution)/shard_map/pj,fsjc->fspc/dot_general | solution.py:50
  134.6 0.5 subtract_bitcast_fusion
  135.1 3.8 %multiply_bitcast_fusion = f32[2,512,512]{2,1,0:T(8,128)S(1)} fusion(f32[2,256,512]{2,1,0:T(8,128)S(1)} %get-tuple-element.8, f32[2,256,512]{2,1,0:T(8,128)S(1)} %get-tuple-element.7, f32[256,256]{1,0:T(8,128)S(1)} %get-tuple-element.23, f32[256,256]{1,0:T(8,128)S(1)} %get-tuple-element.22, f32[256,256]{1,0:T(8,128)S(1)} %fusion.72), kind=kOutput, calls=%fused_computation.21 | convolution fusion | flops 3223060480 | bytes 4980736 | tf_op jit(solution)/shard_map/jp,spc->sjc/dot_general | solution.py:68
  138.9 0.3 fusion.43
  139.4 0.0 copy-start.3
  139.4 29.6 %all_to_all.36 = bf16[8,2,2,32,512]{4,3,2,1,0:T(8,128)(2,1)S(1)} all-to-all(bf16[8,2,2,32,512]{4,3,2,1,0:T(8,128)(2,1)S(1)} %fusion.69), channel_id=1, replica_groups=mesh['ctx'=8,'chan'=4] {'ctx'}, dimensions={0} | all-to-all | bytes 2097152 | tf_op jit(solution)/shard_map/all_to_all | solution.py:113
  169.0 0.1 fusion.120
  169.1 0.6 fusion.49
  169.7 0.6 fusion.32
  170.3 0.1 copy.52
  170.4 12.0 %all_to_all.37 = bf16[8,32,512]{2,1,0:T(8,128)(2,1)S(1)} all-to-all(bf16[8,32,512]{2,1,0:T(8,128)(2,1)S(1)} %copy.52), channel_id=1, replica_groups=mesh['ctx'=8,'chan'=4] {'ctx'}, dimensions={0} | all-to-all | bytes 524288 | tf_op jit(solution)/shard_map/all_to_all | solution.py:126
  182.4 0.0 copy-done.3
  182.4 2.6 %convolution_convert_fusion = bf16[256,4096]{1,0:T(8,128)(2,1)} fusion(bf16[512,4096]{1,0:T(8,128)(2,1)S(1)} %copy-done.3, f32[3,256,512]{2,1,0:T(8,128)S(1)} %copy-done.1, bf16[256,512]{1,0:T(8,128)(2,1)S(1)} %bitcast.122), kind=kOutput, calls=%fused_computation.3 | convolution fusion | flops 1075183616 | bytes 7077888 | tf_op jit(solution)/shard_map/dot_general | solution.py:173
  185.0 0.0 reduce-scatter.2.cloned.1.call-update
  185.1 29.6 %reduce-scatter.2.cloned.1.call-done = bf16[256,1024]{1,0:T(8,128)(2,1)} async-done(((bf16[256,4096]{1,0:T(8,128)(2,1)}), bf16[256,1024]{1,0:T(8,128)(2,1)}) %reduce-scatter.2.cloned.1.call-update) | async-done | bytes 524304 | tf_op jit(solution)/shard_map/reduce_scatter | solution.py:174
  (18 shorter events, 0.1 us)
Async XLA Ops:
  6.5 27.7 %all-gather.2.cloned.1.call-start = ((), (), s32[]{:S(2)}) async-start(), calls=%async_computation.5 | async-start | bytes 2621440 | tf_op jit(solution)/shard_map/all_gather | solution.py:133
  9.0 27.5 %copy-start.4 = (f32[4096]{0:T(1024)S(1)}, f32[4096]{0:T(1024)}, u32[]{:S(2)}) copy-start(f32[4096]{0:T(1024)} %param.8) | copy-start | bytes 49156
  34.2 2.3 %copy-start.2 = (bf16[256,4096]{1,0:T(8,128)(2,1)S(1)}, bf16[256,4096]{1,0:T(8,128)(2,1)}, u32[]{:S(2)}) copy-start(bf16[256,4096]{1,0:T(8,128)(2,1)} %all-gather.2.cloned.1.call-done) | copy-start | bytes 6291460
  43.1 4.7 %collective-permute-start = (bf16[3,2,512]{2,1,0:T(2,128)(2,1)S(1)}, bf16[3,2,512]{2,1,0:T(2,128)(2,1)S(1)}, u32[]{:S(2)}, u32[]{:S(2)}) collective-permute-start(bf16[3,2,512]{2,1,0:T(2,128)(2,1)S(1)} %slice.90), channel_id=1, source_target_pairs={{0,4},{4,8},{8,12},{12,16},{16,20},{20,24},{24,28},{1,5},{5,9},{9,... | collective-permute-start | bytes 18440 | tf_op jit(solution)/shard_map/ppermute | solution.py:22
  48.5 20.6 %copy-start = (f32[3,256,512]{2,1,0:T(8,128)}, f32[3,256,512]{2,1,0:T(8,128)S(1)}, u32[]{:S(2)}) copy-start(f32[3,256,512]{2,1,0:T(8,128)S(1)} %fusion.21) | copy-start | bytes 4718596
  74.1 51.4 %all-to-all-start.1 = ((bf16[2,2,16,32,512]{4,3,0,1,2:T(8,128)(2,1)}), bf16[2,2,16,32,512]{4,3,0,1,2:T(8,128)(2,1)S(1)}, u32[]{:S(2)}, u32[]{:S(2)}) async-start(bf16[2,2,16,32,512]{4,3,0,1,2:T(8,128)(2,1)} %copy.48), calls=%async_computation.1 | async-start | bytes 4194304 | tf_op jit(solution)/shard_map/all_to_all | solution.py:103
  77.8 136.9 %reduce-scatter.2.cloned.1.call-start = ((), (), s32[]{:S(2)}) async-start(), calls=%async_computation.6 | async-start | bytes 2621440 | tf_op jit(solution)/shard_map/reduce_scatter | solution.py:174
  139.4 43.0 %copy-start.3 = (bf16[512,4096]{1,0:T(8,128)(2,1)S(1)}, bf16[512,4096]{1,0:T(8,128)(2,1)}, u32[]{:S(2)}) copy-start(bf16[512,4096]{1,0:T(8,128)(2,1)} %param.13) | copy-start | bytes 12582916
  169.1 13.3 %copy-start.1 = (f32[3,256,512]{2,1,0:T(8,128)S(1)}, f32[3,256,512]{2,1,0:T(8,128)}, u32[]{:S(2)}) copy-start(f32[3,256,512]{2,1,0:T(8,128)} %copy-done) | copy-start | bytes 4718596
Sparse Core Ops, SparseCore 0:
  8.9 25.2 all-gather.1
  185.2 29.4 reduce-scatter.1
